TPU v7x, 128 devices: a whole 4x4x4 slice. The times are simulated.
128 devices in a mesh: ctx: 32 (over x, y, core), head: 4 (over z).
Axes of the slice: x: 4, y: 4, z: 4, core: 2. Of those that a mesh axis runs over, the one named last changes fastest.
Arguments:
- features_in: bfloat16 [16384, 8192], P('ctx', 'head'), may hold values from -6 to 6
- gate_input: bfloat16 [16384, 8192], P('ctx', 'head'), may hold values from -6 to 6
- state_proj: bfloat16 [16384, 256], P('ctx'), may hold values from -6 to 6
- step_raw: float32 [16384, 128], P('ctx', 'head'), may hold values from -2.1 to 2.1, as said below
- rate_log: float32 [128], P('head'), may hold values from -13 to -2.7, as said below
- conv_features: float32 [4, 8192], P(None, 'head'), may hold values from -3 to 3
- conv_states: float32 [4, 256], replicated, may hold values from -3 to 3
- norm_gain: float32 [8192], P('head'), may hold values from 0.25 to 1.75
- out_weight: bfloat16 [8192, 4096], P('head'), may hold values from -0.09375 to 0.09375
Outputs:
- layer_out: bfloat16 [16384, 4096], P('ctx', 'head')
Inputs may be any that keep to these rules, and one draw needn't show every extreme that they name: `rate_log`: per head a decay rate, drawn for each head from one of two ranges: some heads forget within tens of tokens, others keep much of their state over the whole sequence. `step_raw`: varies from token to token and from block to block of tokens.
All inputs are finite; a program needn't handle non-finite values.
Results may differ from a plain program's by a relative error of at most 0.013.
Values may be sent and summed in bfloat16 or wider, within the bound.
A program may use at most 192 MiB of HBM per device.

v0:
```python
import functools

import jax
import jax.numpy as jnp
from jax import lax
from jax.experimental import pallas as pl
from jax.experimental.pallas import tpu as pltpu
from jax.sharding import PartitionSpec as P

HEAD_DIM = 64
STATE = 128
MESH = pl.DeviceIdType.MESH
F32 = jnp.float32
BF16 = jnp.bfloat16

LEAD = 16
ROWS = 64
BLOCK = 128
COLS = 256
SLAB = 64


def dot(a, b):
    return jnp.dot(a, b, preferred_element_type=F32)


def silu(x):
    half = 0.5 * x
    return half + half * jnp.tanh(half)


def iota(shape, axis):
    return lax.broadcasted_iota(jnp.int32, shape, axis)


def in_three(value, group):
    high = value.astype(BF16).astype(F32)
    rest = value - high
    mid = rest.astype(BF16).astype(F32)
    low = rest - mid
    none = jnp.zeros_like(value)
    parts = jnp.where(group == 0, high, jnp.where(group == 1, mid, jnp.where(group == 2, low, none)))
    return parts.astype(BF16)


def layer(
    nctx,
    nhead,
    feat_h,
    gate_h,
    st_h,
    step_h,
    rate_h,
    taps_h,
    staps_h,
    gain_h,
    w_h,
    out_h,
    featb,
    gateb,
    stb,
    bordf,
    bords,
    stepb,
    rateb,
    tapsb,
    stapsb,
    gainb,
    wb,
    ab,
    yb,
    xb,
    db,
    kb,
    qb,
    kt,
    mb,
    a3,
    e3,
    oh,
    oht,
    rowsb,
    tot,
    fade,
    slab_s,
    slab_r,
    ret_s,
    inc,
    rel_s,
    rel_r,
    p_s,
    p_r,
    r_s,
    r_r,
    own,
    lsem,
    bsem,
    ts,
    tr,
    fs,
    fr,
    gs,
    gr,
    js,
    jr,
):
    tokens, feats = gate_h.shape
    half_t = tokens // 2
    outs = out_h.shape[1]
    half_o = outs // 2
    ncb = feats // COLS
    nrow = tokens // ROWS
    nblk = tokens // BLOCK
    me = lax.axis_index("ctx")
    z = lax.axis_index("head")

    loads = [
        (step_h, stepb),
        (rate_h, rateb),
        (taps_h, tapsb),
        (feat_h, featb.at[pl.ds(LEAD, tokens), :]),
        (st_h, stb.at[pl.ds(LEAD, tokens), :]),
        (staps_h, stapsb),
        (gate_h, gateb),
        (gain_h, gainb),
        (w_h, wb),
    ]
    loads = [pltpu.make_async_copy(s, d, lsem.at[i]) for i, (s, d) in enumerate(loads)]
    for load in loads[:6]:
        load.start()

    barrier = pltpu.get_barrier_semaphore()

    def greet(k, _):
        pl.semaphore_signal(
            barrier, inc=1, device_id={"ctx": lax.rem(me + k, nctx)}, device_id_type=MESH
        )
        return 0

    lax.fori_loop(1, nctx, greet, 0)
    for k in (1, nhead - 1):
        pl.semaphore_signal(
            barrier, inc=1, device_id={"head": lax.rem(z + k, nhead)}, device_id_type=MESH
        )

    group = iota((tokens, 128), 1) // 32
    loads[0].wait()
    loads[1].wait()
    raw = jnp.concatenate([stepb[...]] * 4, axis=0).T
    step = jnp.maximum(raw, 0.0) + jnp.log(1.0 + jnp.exp(-jnp.abs(raw)))
    rate = jnp.concatenate([rateb[...]] * 4, axis=1)
    decay = in_three(-step * jnp.exp(rate), group)
    tri = jnp.where(iota((tokens, tokens), 0) >= iota((tokens, tokens), 1), 1.0, 0.0).astype(BF16)
    thirds = dot(tri, decay)
    cum = (
        thirds
        + pltpu.roll(thirds, 32, 1)
        + pltpu.roll(thirds, 64, 1)
        + pltpu.roll(thirds, 96, 1)
    )
    tot[me] = cum[tokens - 1 : tokens]
    centre = cum[half_t - 1 : half_t]
    total = cum[tokens - 1 : tokens]
    away = cum - centre
    a3[...] = in_three(step * jnp.exp(-away), group)
    e3[...] = in_three(jnp.exp(away), group)
    oh[...] = jnp.where((iota((128, feats), 0) & 31) == iota((128, feats), 1) // HEAD_DIM, 1.0, 0.0).astype(BF16)
    oht[...] = jnp.where(
        (iota((feats, 128), 1) & 31) == iota((feats, 128), 0) // HEAD_DIM, 1.0 / HEAD_DIM, 0.0
    ).astype(BF16)
    line = iota((16, 128), 0)
    scales = jnp.where(line == 0, jnp.exp(total - centre), jnp.exp(centre))
    rowsb[...] = dot(in_three(scales, iota((16, 128), 1) // 32), oh[...])

    def conv(x, taps):
        total = x * taps[3:4]
        for back in range(1, 4):
            total = total + pltpu.roll(x, back, 0) * taps[3 - back : 4 - back]
        return silu(total[LEAD:])

    def columns(cb):
        return pl.ds(pl.multiple_of(cb * COLS, COLS), COLS)

    featb[0:LEAD, :] = jnp.zeros((LEAD, feats), BF16)
    stb[0:LEAD, :] = jnp.zeros((LEAD, 2 * STATE), BF16)
    loads[2].wait()
    loads[3].wait()
    for load in loads[6:]:
        load.start()

    def feature_block(cb, _):
        cols = columns(cb)
        ab[:, cols] = dot(a3[...], oh[:, cols])

        def chunk(r, _):
            at = pl.multiple_of(r * ROWS, ROWS)
            x = featb[pl.ds(at, ROWS + LEAD), cols].astype(F32)
            v = conv(x, tapsb[:, cols]) * ab[pl.ds(at, ROWS), cols]
            xb[pl.ds(at, ROWS), cols] = v.astype(BF16)
            return 0

        return lax.fori_loop(0, nrow, chunk, 0, unroll=True)

    lax.fori_loop(0, ncb, feature_block, 0)
    loads[4].wait()
    loads[5].wait()

    def states(r, _):
        at = pl.multiple_of(r * ROWS, ROWS)
        v = conv(stb[pl.ds(at, ROWS + LEAD), :].astype(F32), stapsb[...])
        kb[pl.ds(at, ROWS), :] = v[:, :STATE].astype(BF16).astype(F32)
        qb[pl.ds(at, ROWS), :] = v[:, STATE:].astype(BF16)
        return 0

    lax.fori_loop(0, nrow, states, 0, unroll=True)
    later = iota((tokens, STATE), 0) >= LEAD
    kt[...] = jnp.where(later, kb[...], 0.0).T.astype(BF16)

    def state_block(cb, _):
        cols = columns(cb)
        db[:, cols] = dot(kt[...], xb[:, cols])
        return 0

    lax.fori_loop(0, ncb, state_block, 0, unroll=2)

    pl.semaphore_wait(barrier, nctx + 1)
    after = lax.rem(me + 1, nctx)
    borders = [
        pltpu.make_async_remote_copy(
            src_ref=src.at[pl.ds(tokens, LEAD), :],
            dst_ref=dst,
            send_sem=bsem.at[i],
            recv_sem=bsem.at[2 + i],
            device_id={"ctx": after},
            device_id_type=MESH,
        )
        for i, (src, dst) in enumerate(((featb, bordf), (stb, bords)))
    ]

    @pl.when(me < nctx - 1)
    def _():
        for border in borders:
            border.start()

    @pl.when(me == 0)
    def _():
        bordf[...] = jnp.zeros((LEAD, feats), BF16)
        bords[...] = jnp.zeros((LEAD, 2 * STATE), BF16)

    def total_copy(slot, to):
        return pltpu.make_async_remote_copy(
            src_ref=tot.at[slot],
            dst_ref=tot.at[slot],
            send_sem=ts.at[to],
            recv_sem=tr.at[slot],
            device_id={"ctx": to},
            device_id_type=MESH,
        )

    def send_total(k, _):
        total_copy(me, lax.rem(me + k, nctx)).start()
        return 0

    lax.fori_loop(1, nctx, send_total, 0)

    @pl.when(me > 0)
    def _():
        for border in borders:
            border.wait_recv()

    v = conv(jnp.concatenate([bords[...], stb[LEAD : 2 * LEAD, :]], axis=0).astype(F32), stapsb[...])
    kb[0:LEAD, :] = v[:, :STATE].astype(BF16).astype(F32)
    qb[0:LEAD, :] = v[:, STATE:].astype(BF16)
    for cb in range(ncb):
        cols = slice(cb * COLS, (cb + 1) * COLS)
        x = jnp.concatenate([bordf[:, cols], featb[LEAD : 2 * LEAD, cols]], axis=0).astype(F32)
        xb[0:LEAD, cols] = (conv(x, tapsb[:, cols]) * ab[0:LEAD, cols]).astype(BF16)

    first = jnp.where(iota((128, STATE), 0) < LEAD, kb[0:128, :], 0.0).T.astype(BF16)

    def slab_copy(src, slot, to):
        return pltpu.make_async_remote_copy(
            src_ref=slab_s.at[src],
            dst_ref=slab_r.at[slot],
            send_sem=fs.at[src],
            recv_sem=fr.at[slot],
            device_id={"ctx": to},
            device_id_type=MESH,
        )

    for part in range(2):
        rows = slice(part * SLAB, (part + 1) * SLAB)
        for cb in range(ncb):
            cols = slice(cb * COLS, (cb + 1) * COLS)
            d = db[rows, cols] + dot(first[rows], xb[0:128, cols])
            d = (d * rowsb[0:1, cols]).astype(BF16)
            for pair in range(COLS // 128):
                slab_s[(cb * (COLS // 128) + pair) * 2 + part] = d[:, pair * 128 : pair * 128 + 128]

        def send_slab(k, _):
            to = 2 * lax.rem(me // 2 + k, nctx // 2) + part

            @pl.when(to != me)
            def _():
                slab_copy(to, me, to).start()

            return 0

        lax.fori_loop(0, nctx // 2, send_slab, 0)
    slab_r[me] = slab_s[me]
    kt[...] = kb[...].T.astype(BF16)

    for i in range(2):
        score = dot(qb[i * half_t : (i + 1) * half_t, :], kt[...])
        keep = iota((half_t, tokens), 0) + i * half_t >= iota((half_t, tokens), 1)
        mb[i * half_t : (i + 1) * half_t, :] = jnp.where(keep, score, 0.0).astype(BF16)

    def intra(cb, _):
        cols = columns(cb)
        yb[0:half_t, cols] = dot(mb[0:half_t, 0:half_t], xb[0:half_t, cols])
        yb[half_t:tokens, cols] = dot(mb[half_t:tokens, :], xb[:, cols])
        return 0

    lax.fori_loop(0, ncb, intra, 0)

    def back_copy(src, owner, to):
        rows = pl.ds(pl.multiple_of(lax.rem(owner, 2) * SLAB, SLAB), SLAB)
        lanes = pl.ds(pl.multiple_of((owner // 2) * 128, 128), 128)
        return pltpu.make_async_remote_copy(
            src_ref=ret_s.at[src],
            dst_ref=inc.at[rows, lanes],
            send_sem=gs.at[src],
            recv_sem=gr.at[owner],
            device_id={"ctx": to},
            device_id_type=MESH,
        )

    def total_here(e, _):
        @pl.when(e != me)
        def _():
            total_copy(e, e).wait_recv()

        return 0

    lax.fori_loop(0, nctx, total_here, 0)
    lanes = pl.ds(pl.multiple_of((me // 2) * 128, 128), 128)
    everyone = in_three(tot[...].reshape(nctx, 128), iota((nctx, 128), 1) // 32)
    fade[...] = jnp.exp(dot(everyone, oh[:, lanes])).reshape(nctx, 1, 128)

    def slab_here(e, _):
        @pl.when(e != me)
        def _():
            slab_copy(e, e, e).wait_recv()

        return 0

    lax.fori_loop(0, nctx, slab_here, 0)

    def scan(i, run):
        for e in range(8):
            ret_s[i * 8 + e] = run.astype(BF16)
            run = fade[i * 8 + e] * run + slab_r[i * 8 + e].astype(F32)
        return run

    lax.fori_loop(0, nctx // 8, scan, jnp.zeros((SLAB, 128), F32))

    def send_back(k, _):
        to = lax.rem(me + k, nctx)
        back_copy(to, me, to).start()
        return 0

    lax.fori_loop(1, nctx, send_back, 0)
    inc[
        pl.ds(pl.multiple_of(lax.rem(me, 2) * SLAB, SLAB), SLAB),
        pl.ds(pl.multiple_of((me // 2) * 128, 128), 128),
    ] = ret_s[me]

    loads[6].wait()

    def gate_block(i, _):
        cols = columns(i // 4)
        at = pl.ds(pl.multiple_of(lax.rem(i, 4) * 128, 128), 128)
        ab[at, cols] = dot(e3[at, :], oh[:, cols]) * silu(gateb[at, cols].astype(F32))
        return 0

    lax.fori_loop(0, ncb * 4, gate_block, 0)
    loads[7].wait()
    loads[8].wait()

    def arrived(e, _):
        @pl.when(e != me)
        def _():
            back_copy(e, e, e).wait_recv()

        return 0

    lax.fori_loop(0, nctx, arrived, 0)

    group_n = iota((BLOCK, 128), 1) // 32

    def block_rows(b):
        return pl.ds(pl.multiple_of(b * BLOCK, BLOCK), BLOCK)

    def norm_block(b):
        at = block_rows(b)
        mean = jnp.zeros((BLOCK, 128), F32)
        for cb in range(ncb):
            cols = slice(cb * COLS, (cb + 1) * COLS)
            y = dot(qb[at, :], inc[:, cols]) * rowsb[1:2, cols] + yb[at, cols]
            y = y * ab[at, cols]
            yb[at, cols] = y
            mean = mean + dot((y * y).astype(BF16), oht[cols, :])
        scale = in_three(lax.rsqrt(mean + 1e-05), group_n)
        for cb in range(ncb):
            cols = slice(cb * COLS, (cb + 1) * COLS)
            xb[at, cols] = (yb[at, cols] * dot(scale, oh[:, cols]) * gainb[:, cols]).astype(BF16)

    def project(b, dest, half):
        cols = pl.ds(pl.multiple_of(dest * outs + half * half_o, half_o), half_o)
        return dot(xb[block_rows(b), :], wb[:, cols])

    def towards(side):
        return lax.rem(z + 1 + side * (nhead - 2), nhead)

    def job_copy(src, dst, side, b, first):
        i = (first * nblk + b) * 2 + side
        return pltpu.make_async_remote_copy(
            src_ref=src.at[side, b],
            dst_ref=dst.at[side, b],
            send_sem=js.at[i],
            recv_sem=jr.at[i],
            device_id={"head": towards(side)},
            device_id_type=MESH,
        )

    def relay_block(b, _):
        norm_block(b)

        def one(side, _):
            rel_s[side, b] = project(b, lax.rem(z + 2, nhead), side).astype(BF16)
            job_copy(rel_s, rel_r, side, b, 0).start()
            return 0

        return lax.fori_loop(0, 2, one, 0)

    lax.fori_loop(0, nblk, relay_block, 0)

    def plain(i, _):
        b, side = i // 2, lax.rem(i, 2)
        p_s[side, b] = project(b, towards(side), 1 - side).astype(BF16)
        job_copy(p_s, p_r, side, b, 1).start()
        return 0

    lax.fori_loop(0, 2 * nblk, plain, 0)

    def relayed(i, _):
        b, side = i // 2, lax.rem(i, 2)
        part = project(b, towards(side), side)
        job_copy(rel_s, rel_r, side, b, 0).wait_recv()
        r_s[side, b] = (part + rel_r[side, b].astype(F32)).astype(BF16)
        job_copy(r_s, r_r, side, b, 2).start()
        return 0

    lax.fori_loop(0, 2 * nblk, relayed, 0)

    def mine(i, _):
        b, half = i // 2, lax.rem(i, 2)
        own[half, b] = project(b, z, half)
        return 0

    lax.fori_loop(0, 2 * nblk, mine, 0)

    @pl.when(me < nctx - 1)
    def _():
        for border in borders:
            border.wait_send()

    def left(k, _):
        to = lax.rem(me + k, nctx)
        slab_copy(to, me, to).wait_send()
        back_copy(to, me, to).wait_send()
        total_copy(me, to).wait_send()
        return 0

    lax.fori_loop(1, nctx, left, 0)

    def jobs_left(i, _):
        b, side = i // 2, lax.rem(i, 2)
        job_copy(rel_s, rel_r, side, b, 0).wait_send()
        job_copy(p_s, p_r, side, b, 1).wait_send()
        return 0

    lax.fori_loop(0, 2 * nblk, jobs_left, 0)

    def finish(i, _):
        b, half = i // 2, lax.rem(i, 2)
        job_copy(p_s, p_r, 1 - half, b, 1).wait_recv()
        job_copy(r_s, r_r, half, b, 2).wait_send()
        job_copy(r_s, r_r, half, b, 2).wait_recv()
        total = own[half, b] + p_r[1 - half, b].astype(F32) + r_r[half, b].astype(F32)
        out_h[block_rows(b), pl.ds(pl.multiple_of(half * half_o, half_o), half_o)] = total.astype(BF16)
        return 0

    lax.fori_loop(0, 2 * nblk, finish, 0)


def per_device(
    nctx,
    nhead,
    features_in,
    gate_input,
    state_proj,
    step_raw,
    rate_log,
    conv_features,
    conv_states,
    norm_gain,
    out_weight,
):
    tokens, feats = features_in.shape
    heads = rate_log.shape[0]
    outs = out_weight.shape[1] // nhead
    half_o = outs // 2
    any_space = pl.BlockSpec(memory_space=pltpu.HBM)
    vmem = pltpu.VMEM
    dma = pltpu.SemaphoreType.DMA
    job = (2, tokens // BLOCK, BLOCK, half_o)
    scratch = [
        vmem((LEAD + tokens, feats), BF16),
        vmem((tokens, feats), BF16),
        vmem((LEAD + tokens, 2 * STATE), BF16),
        vmem((LEAD, feats), BF16),
        vmem((LEAD, 2 * STATE), BF16),
        vmem((heads, tokens), F32),
        vmem((1, heads), F32),
        vmem((4, feats), F32),
        vmem((4, 2 * STATE), F32),
        vmem((1, feats), F32),
        vmem(out_weight.shape, BF16),
        vmem((tokens, feats), F32),
        vmem((tokens, feats), F32),
        vmem((tokens, feats), BF16),
        vmem((STATE, feats), F32),
        vmem((tokens, STATE), F32),
        vmem((tokens, STATE), BF16),
        vmem((STATE, tokens), BF16),
        vmem((tokens, tokens), BF16),
        vmem((tokens, 128), BF16),
        vmem((tokens, 128), BF16),
        vmem((128, feats), BF16),
        vmem((feats, 128), BF16),
        vmem((16, feats), F32),
        vmem((nctx, 1, 128), F32),
        vmem((nctx, 1, 128), F32),
        vmem((nctx, SLAB, 128), BF16),
        vmem((nctx, SLAB, 128), BF16),
        vmem((nctx, SLAB, 128), BF16),
        vmem((STATE, feats), BF16),
        vmem(job, BF16),
        vmem(job, BF16),
        vmem(job, BF16),
        vmem(job, BF16),
        vmem(job, BF16),
        vmem(job, BF16),
        vmem(job, F32),
        dma((9,)),
        dma((4,)),
        dma((nctx,)),
        dma((nctx,)),
        dma((nctx,)),
        dma((nctx,)),
        dma((nctx,)),
        dma((nctx,)),
        dma((6 * (tokens // BLOCK),)),
        dma((6 * (tokens // BLOCK),)),
    ]
    return pl.pallas_call(
        functools.partial(layer, nctx, nhead),
        out_shape=jax.ShapeDtypeStruct((tokens, outs), BF16),
        in_specs=[any_space] * 9,
        out_specs=pl.BlockSpec(memory_space=pltpu.VMEM),
        scratch_shapes=scratch,
        compiler_params=pltpu.CompilerParams(collective_id=0, has_side_effects=True, vmem_limit_bytes=52 * 1024 * 1024),
        name="ssd_layer",
    )(
        *(
            pltpu.with_memory_space_constraint(a, pltpu.HBM)
            for a in (
                features_in,
                gate_input,
                state_proj,
                step_raw.T,
                rate_log.reshape(1, heads),
                conv_features,
                conv_states,
                norm_gain.reshape(1, feats),
                out_weight,
            )
        )
    )


def solution(mesh):
    placed = (
        P("ctx", "head"),
        P("ctx", "head"),
        P("ctx", None),
        P("ctx", "head"),
        P("head"),
        P(None, "head"),
        P(),
        P("head"),
        P("head", None),
    )
    body = functools.partial(per_device, mesh.shape["ctx"], mesh.shape["head"])
    return jax.shard_map(
        body, mesh=mesh, in_specs=placed, out_specs=P("ctx", "head"), check_vma=False
    )
```

profile of v0, /device:TPU:1, one launch (start us, length us, event | category | flops | bytes accessed | tf_op | source)
XLA Modules:
  0.0 71.8 jit_solution(16118294657256925706)
XLA Ops:
  0.0 70.8 %ssd_layer.1 = bf16[512,1024]{1,0:T(8,128)(2,1)S(1)} custom-call(bf16[512,2048]{1,0:T(8,128)(2,1)} %feat_h.1, bf16[512,2048]{1,0:T(8,128)(2,1)} %gate_h.1, bf16[512,256]{1,0:T(8,128)(2,1)} %st_h.1, f32[32,512]{1,0:T(8,128)} %bitcast.3, f32[1,32]{1,0:T(1,128)} %bitcast.5, f32[4,2048]{1,0:T(4,128)} %taps_h.1, f32[4,256]{1,0:T(4,128)} %staps_h.1, ...), custom_call_target="tpu_custom_call" | custom-call | tf_op jit(solution)/shard_map/ssd_layer/pallas_call | solution.py:577
  70.8 1.0 %copy.11 = bf16[512,1024]{1,0:T(8,128)(2,1)} copy(bf16[512,1024]{1,0:T(8,128)(2,1)S(1)} %ssd_layer.1) | data formatting | bytes 2097152
where the time goes:
time: 71.9 us; the launch traced here: 71.8 us
  Pallas kernels  70.8 us (98%)
  local copies, waits for them, and re-layouts  0.97 us (1%)
    pallas_call x1, Pallas kernels, per_device(): pl.pallas_call(functools.partial(layer, nctx, nhead), out_shape=jax.Shape...  70.8 us

commit v1 on v0

--- a/solution.py
+++ b/solution.py
@@ -95,12 +95,7 @@
     own,
     lsem,
     bsem,
-    ts,
-    tr,
-    fs,
-    fr,
-    gs,
-    gr,
+    csem,
     js,
     jr,
 ):
@@ -117,10 +112,10 @@
     loads = [
         (step_h, stepb),
         (rate_h, rateb),
+        (st_h, stb.at[pl.ds(LEAD, tokens), :]),
+        (staps_h, stapsb),
         (taps_h, tapsb),
         (feat_h, featb.at[pl.ds(LEAD, tokens), :]),
-        (st_h, stb.at[pl.ds(LEAD, tokens), :]),
-        (staps_h, stapsb),
         (gate_h, gateb),
         (gain_h, gainb),
         (w_h, wb),
@@ -144,13 +139,19 @@
         )
 
     group = iota((tokens, 128), 1) // 32
+    tri = jnp.where(iota((tokens, tokens), 0) >= iota((tokens, tokens), 1), 1.0, 0.0).astype(BF16)
+    oh[...] = jnp.where((iota((128, feats), 0) & 31) == iota((128, feats), 1) // HEAD_DIM, 1.0, 0.0).astype(BF16)
+    oht[...] = jnp.where(
+        (iota((feats, 128), 1) & 31) == iota((feats, 128), 0) // HEAD_DIM, 1.0 / HEAD_DIM, 0.0
+    ).astype(BF16)
+    featb[0:LEAD, :] = jnp.zeros((LEAD, feats), BF16)
+    stb[0:LEAD, :] = jnp.zeros((LEAD, 2 * STATE), BF16)
     loads[0].wait()
     loads[1].wait()
     raw = jnp.concatenate([stepb[...]] * 4, axis=0).T
     step = jnp.maximum(raw, 0.0) + jnp.log(1.0 + jnp.exp(-jnp.abs(raw)))
     rate = jnp.concatenate([rateb[...]] * 4, axis=1)
     decay = in_three(-step * jnp.exp(rate), group)
-    tri = jnp.where(iota((tokens, tokens), 0) >= iota((tokens, tokens), 1), 1.0, 0.0).astype(BF16)
     thirds = dot(tri, decay)
     cum = (
         thirds
@@ -164,10 +165,6 @@
     away = cum - centre
     a3[...] = in_three(step * jnp.exp(-away), group)
     e3[...] = in_three(jnp.exp(away), group)
-    oh[...] = jnp.where((iota((128, feats), 0) & 31) == iota((128, feats), 1) // HEAD_DIM, 1.0, 0.0).astype(BF16)
-    oht[...] = jnp.where(
-        (iota((feats, 128), 1) & 31) == iota((feats, 128), 0) // HEAD_DIM, 1.0 / HEAD_DIM, 0.0
-    ).astype(BF16)
     line = iota((16, 128), 0)
     scales = jnp.where(line == 0, jnp.exp(total - centre), jnp.exp(centre))
     rowsb[...] = dot(in_three(scales, iota((16, 128), 1) // 32), oh[...])
@@ -181,14 +178,26 @@
     def columns(cb):
         return pl.ds(pl.multiple_of(cb * COLS, COLS), COLS)
 
-    featb[0:LEAD, :] = jnp.zeros((LEAD, feats), BF16)
-    stb[0:LEAD, :] = jnp.zeros((LEAD, 2 * STATE), BF16)
     loads[2].wait()
     loads[3].wait()
+
+    def states(r, _):
+        at = pl.multiple_of(r * ROWS, ROWS)
+        v = conv(stb[pl.ds(at, ROWS + LEAD), :].astype(F32), stapsb[...])
+        kb[pl.ds(at, ROWS), :] = v[:, :STATE].astype(BF16).astype(F32)
+        qb[pl.ds(at, ROWS), :] = v[:, STATE:].astype(BF16)
+        return 0
+
+    lax.fori_loop(0, nrow, states, 0, unroll=True)
+    later = iota((tokens, STATE), 0) >= LEAD
+    kt[...] = jnp.where(later, kb[...], 0.0).T.astype(BF16)
+
+    loads[4].wait()
+    loads[5].wait()
     for load in loads[6:]:
         load.start()
 
-    def feature_block(cb, _):
+    def feature_block(cb):
         cols = columns(cb)
         ab[:, cols] = dot(a3[...], oh[:, cols])
 
@@ -199,29 +208,19 @@
             xb[pl.ds(at, ROWS), cols] = v.astype(BF16)
             return 0
 
-        return lax.fori_loop(0, nrow, chunk, 0, unroll=True)
-
-    lax.fori_loop(0, ncb, feature_block, 0)
-    loads[4].wait()
-    loads[5].wait()
-
-    def states(r, _):
-        at = pl.multiple_of(r * ROWS, ROWS)
-        v = conv(stb[pl.ds(at, ROWS + LEAD), :].astype(F32), stapsb[...])
-        kb[pl.ds(at, ROWS), :] = v[:, :STATE].astype(BF16).astype(F32)
-        qb[pl.ds(at, ROWS), :] = v[:, STATE:].astype(BF16)
-        return 0
-
-    lax.fori_loop(0, nrow, states, 0, unroll=True)
-    later = iota((tokens, STATE), 0) >= LEAD
-    kt[...] = jnp.where(later, kb[...], 0.0).T.astype(BF16)
-
-    def state_block(cb, _):
+        lax.fori_loop(0, nrow, chunk, 0, unroll=True)
+
+    def state_block(cb):
         cols = columns(cb)
         db[:, cols] = dot(kt[...], xb[:, cols])
-        return 0
-
-    lax.fori_loop(0, ncb, state_block, 0, unroll=2)
+
+    def both(cb, _):
+        state_block(cb - 1)
+        feature_block(cb)
+        return 0
+
+    feature_block(0)
+    lax.fori_loop(1, ncb // 2, both, 0)
 
     pl.semaphore_wait(barrier, nctx + 1)
     after = lax.rem(me + 1, nctx)
@@ -247,21 +246,8 @@
         bordf[...] = jnp.zeros((LEAD, feats), BF16)
         bords[...] = jnp.zeros((LEAD, 2 * STATE), BF16)
 
-    def total_copy(slot, to):
-        return pltpu.make_async_remote_copy(
-            src_ref=tot.at[slot],
-            dst_ref=tot.at[slot],
-            send_sem=ts.at[to],
-            recv_sem=tr.at[slot],
-            device_id={"ctx": to},
-            device_id_type=MESH,
-        )
-
-    def send_total(k, _):
-        total_copy(me, lax.rem(me + k, nctx)).start()
-        return 0
-
-    lax.fori_loop(1, nctx, send_total, 0)
+    lax.fori_loop(ncb // 2, ncb, both, 0)
+    state_block(ncb - 1)
 
     @pl.when(me > 0)
     def _():
@@ -278,15 +264,29 @@
 
     first = jnp.where(iota((128, STATE), 0) < LEAD, kb[0:128, :], 0.0).T.astype(BF16)
 
-    def slab_copy(src, slot, to):
+    def total_copy(to):
         return pltpu.make_async_remote_copy(
-            src_ref=slab_s.at[src],
-            dst_ref=slab_r.at[slot],
-            send_sem=fs.at[src],
-            recv_sem=fr.at[slot],
+            src_ref=tot.at[me],
+            dst_ref=tot.at[me],
+            send_sem=csem.at[0],
+            recv_sem=csem.at[1],
             device_id={"ctx": to},
             device_id_type=MESH,
         )
+
+    def slab_copy(to):
+        return pltpu.make_async_remote_copy(
+            src_ref=slab_s.at[to],
+            dst_ref=slab_r.at[me],
+            send_sem=csem.at[2],
+            recv_sem=csem.at[3],
+            device_id={"ctx": to},
+            device_id_type=MESH,
+        )
+
+    def wait_all(like, i):
+        whole = like.at[pl.ds(0, nctx - 1)]
+        pltpu.make_async_copy(whole, whole, csem.at[i]).wait()
 
     for part in range(2):
         rows = slice(part * SLAB, (part + 1) * SLAB)
@@ -297,16 +297,17 @@
             for pair in range(COLS // 128):
                 slab_s[(cb * (COLS // 128) + pair) * 2 + part] = d[:, pair * 128 : pair * 128 + 128]
 
-        def send_slab(k, _):
-            to = 2 * lax.rem(me // 2 + k, nctx // 2) + part
-
-            @pl.when(to != me)
+        for quarter in (part, part + 2):
+
+            @pl.when(lax.rem(me, 4) != quarter)
             def _():
-                slab_copy(to, me, to).start()
-
-            return 0
-
-        lax.fori_loop(0, nctx // 2, send_slab, 0)
+                slab_copy((me // 4) * 4 + quarter).start()
+
+            for k in range(1, nctx // 4):
+                slab_copy(lax.rem(me // 4 + k, nctx // 4) * 4 + quarter).start()
+        if part == 0:
+            for k in range(1, nctx):
+                total_copy(lax.rem(me + k, nctx)).start()
     slab_r[me] = slab_s[me]
     kt[...] = kb[...].T.astype(BF16)
 
@@ -323,38 +324,24 @@
 
     lax.fori_loop(0, ncb, intra, 0)
 
-    def back_copy(src, owner, to):
-        rows = pl.ds(pl.multiple_of(lax.rem(owner, 2) * SLAB, SLAB), SLAB)
-        lanes = pl.ds(pl.multiple_of((owner // 2) * 128, 128), 128)
+    def back_copy(to):
+        rows = pl.ds(pl.multiple_of(lax.rem(me, 2) * SLAB, SLAB), SLAB)
+        lanes = pl.ds(pl.multiple_of((me // 2) * 128, 128), 128)
         return pltpu.make_async_remote_copy(
-            src_ref=ret_s.at[src],
+            src_ref=ret_s.at[to],
             dst_ref=inc.at[rows, lanes],
-            send_sem=gs.at[src],
-            recv_sem=gr.at[owner],
+            send_sem=csem.at[4],
+            recv_sem=csem.at[5],
             device_id={"ctx": to},
             device_id_type=MESH,
         )
 
-    def total_here(e, _):
-        @pl.when(e != me)
-        def _():
-            total_copy(e, e).wait_recv()
-
-        return 0
-
-    lax.fori_loop(0, nctx, total_here, 0)
+    wait_all(tot, 1)
     lanes = pl.ds(pl.multiple_of((me // 2) * 128, 128), 128)
     everyone = in_three(tot[...].reshape(nctx, 128), iota((nctx, 128), 1) // 32)
     fade[...] = jnp.exp(dot(everyone, oh[:, lanes])).reshape(nctx, 1, 128)
 
-    def slab_here(e, _):
-        @pl.when(e != me)
-        def _():
-            slab_copy(e, e, e).wait_recv()
-
-        return 0
-
-    lax.fori_loop(0, nctx, slab_here, 0)
+    wait_all(slab_r, 3)
 
     def scan(i, run):
         for e in range(8):
@@ -364,12 +351,8 @@
 
     lax.fori_loop(0, nctx // 8, scan, jnp.zeros((SLAB, 128), F32))
 
-    def send_back(k, _):
-        to = lax.rem(me + k, nctx)
-        back_copy(to, me, to).start()
-        return 0
-
-    lax.fori_loop(1, nctx, send_back, 0)
+    for k in range(1, nctx):
+        back_copy(lax.rem(me + k, nctx)).start()
     inc[
         pl.ds(pl.multiple_of(lax.rem(me, 2) * SLAB, SLAB), SLAB),
         pl.ds(pl.multiple_of((me // 2) * 128, 128), 128),
@@ -387,14 +370,7 @@
     loads[7].wait()
     loads[8].wait()
 
-    def arrived(e, _):
-        @pl.when(e != me)
-        def _():
-            back_copy(e, e, e).wait_recv()
-
-        return 0
-
-    lax.fori_loop(0, nctx, arrived, 0)
+    wait_all(ret_s, 5)
 
     group_n = iota((BLOCK, 128), 1) // 32
 
@@ -475,14 +451,9 @@
         for border in borders:
             border.wait_send()
 
-    def left(k, _):
-        to = lax.rem(me + k, nctx)
-        slab_copy(to, me, to).wait_send()
-        back_copy(to, me, to).wait_send()
-        total_copy(me, to).wait_send()
-        return 0
-
-    lax.fori_loop(1, nctx, left, 0)
+    wait_all(tot, 0)
+    wait_all(slab_r, 2)
+    wait_all(ret_s, 4)
 
     def jobs_left(i, _):
         b, side = i // 2, lax.rem(i, 2)
@@ -565,12 +536,7 @@
         vmem(job, F32),
         dma((9,)),
         dma((4,)),
-        dma((nctx,)),
-        dma((nctx,)),
-        dma((nctx,)),
-        dma((nctx,)),
-        dma((nctx,)),
-        dma((nctx,)),
+        dma((6,)),
         dma((6 * (tokens // BLOCK),)),
         dma((6 * (tokens // BLOCK),)),
     ]

time: 71.9 us -> 67.7 us (0.942)
  Pallas kernels: 70.8 us -> 66.6 us
    pallas_call x1, Pallas kernels: 70.8 us -> 66.6 us  [per_device(): pl.pallas_call(functools.partial(layer, nctx, nhead), out_shape=jax.Shape...]
where the time goes in v1:
time: 67.7 us; the launch traced here: 67.6 us
  Pallas kernels  66.6 us (98%)
  local copies, waits for them, and re-layouts  0.97 us (1%)
    pallas_call x1, Pallas kernels, per_device(): pl.pallas_call(functools.partial(layer, nctx, nhead), out_shape=jax.Shape...  66.6 us

profile of v1, /device:TPU:1, one launch (start us, length us, event | category | flops | bytes accessed | tf_op | source)
XLA Modules:
  0.0 67.6 jit_solution(9418554378079332818)
XLA Ops:
  0.0 66.6 %ssd_layer.1 = bf16[512,1024]{1,0:T(8,128)(2,1)S(1)} custom-call(bf16[512,2048]{1,0:T(8,128)(2,1)} %feat_h.1, bf16[512,2048]{1,0:T(8,128)(2,1)} %gate_h.1, bf16[512,256]{1,0:T(8,128)(2,1)} %st_h.1, f32[32,512]{1,0:T(8,128)} %bitcast.3, f32[1,32]{1,0:T(1,128)} %bitcast.5, f32[4,2048]{1,0:T(4,128)} %taps_h.1, f32[4,256]{1,0:T(4,128)} %staps_h.1, ...), custom_call_target="tpu_custom_call" | custom-call | tf_op jit(solution)/shard_map/ssd_layer/pallas_call | solution.py:543
  66.6 1.0 %copy.11 = bf16[512,1024]{1,0:T(8,128)(2,1)} copy(bf16[512,1024]{1,0:T(8,128)(2,1)S(1)} %ssd_layer.1) | data formatting | bytes 2097152

commit v2 on v1

--- a/solution.py
+++ b/solution.py
@@ -18,6 +18,7 @@
 BLOCK = 128
 COLS = 256
 SLAB = 64
+GROUPS = 4
 
 
 def dot(a, b):
@@ -257,11 +258,6 @@
     v = conv(jnp.concatenate([bords[...], stb[LEAD : 2 * LEAD, :]], axis=0).astype(F32), stapsb[...])
     kb[0:LEAD, :] = v[:, :STATE].astype(BF16).astype(F32)
     qb[0:LEAD, :] = v[:, STATE:].astype(BF16)
-    for cb in range(ncb):
-        cols = slice(cb * COLS, (cb + 1) * COLS)
-        x = jnp.concatenate([bordf[:, cols], featb[LEAD : 2 * LEAD, cols]], axis=0).astype(F32)
-        xb[0:LEAD, cols] = (conv(x, tapsb[:, cols]) * ab[0:LEAD, cols]).astype(BF16)
-
     first = jnp.where(iota((128, STATE), 0) < LEAD, kb[0:128, :], 0.0).T.astype(BF16)
 
     def total_copy(to):
@@ -288,24 +284,27 @@
         whole = like.at[pl.ds(0, nctx - 1)]
         pltpu.make_async_copy(whole, whole, csem.at[i]).wait()
 
-    for part in range(2):
-        rows = slice(part * SLAB, (part + 1) * SLAB)
-        for cb in range(ncb):
+    for g in range(GROUPS):
+        for cb in range(g * ncb // GROUPS, (g + 1) * ncb // GROUPS):
             cols = slice(cb * COLS, (cb + 1) * COLS)
-            d = db[rows, cols] + dot(first[rows], xb[0:128, cols])
+            x = jnp.concatenate([bordf[:, cols], featb[LEAD : 2 * LEAD, cols]], axis=0).astype(F32)
+            xb[0:LEAD, cols] = (conv(x, tapsb[:, cols]) * ab[0:LEAD, cols]).astype(BF16)
+            d = db[:, cols] + dot(first, xb[0:128, cols])
             d = (d * rowsb[0:1, cols]).astype(BF16)
             for pair in range(COLS // 128):
-                slab_s[(cb * (COLS // 128) + pair) * 2 + part] = d[:, pair * 128 : pair * 128 + 128]
-
-        for quarter in (part, part + 2):
-
-            @pl.when(lax.rem(me, 4) != quarter)
-            def _():
-                slab_copy((me // 4) * 4 + quarter).start()
-
-            for k in range(1, nctx // 4):
-                slab_copy(lax.rem(me // 4 + k, nctx // 4) * 4 + quarter).start()
-        if part == 0:
+                at = (cb * (COLS // 128) + pair) % 4
+                for part in range(2):
+                    slab_s[(at * 2 + part) * GROUPS + g] = d[
+                        part * SLAB : (part + 1) * SLAB, pair * 128 : pair * 128 + 128
+                    ]
+        for k in range(1, nctx // GROUPS):
+            slab_copy(lax.rem(me // GROUPS + k, nctx // GROUPS) * GROUPS + g).start()
+
+        @pl.when(lax.rem(me, GROUPS) != g)
+        def _():
+            slab_copy((me // GROUPS) * GROUPS + g).start()
+
+        if g == 1:
             for k in range(1, nctx):
                 total_copy(lax.rem(me + k, nctx)).start()
     slab_r[me] = slab_s[me]
@@ -324,22 +323,23 @@
 
     lax.fori_loop(0, ncb, intra, 0)
 
+    group_me = lax.rem(me, GROUPS)
+    my_rows = pl.ds(pl.multiple_of(lax.rem(me // GROUPS, 2) * SLAB, SLAB), SLAB)
+    my_lanes = pl.ds(pl.multiple_of((group_me * 4 + me // (2 * GROUPS)) * 128, 128), 128)
+
     def back_copy(to):
-        rows = pl.ds(pl.multiple_of(lax.rem(me, 2) * SLAB, SLAB), SLAB)
-        lanes = pl.ds(pl.multiple_of((me // 2) * 128, 128), 128)
         return pltpu.make_async_remote_copy(
             src_ref=ret_s.at[to],
-            dst_ref=inc.at[rows, lanes],
+            dst_ref=inc.at[my_rows, my_lanes],
             send_sem=csem.at[4],
-            recv_sem=csem.at[5],
+            recv_sem=csem.at[5 + group_me],
             device_id={"ctx": to},
             device_id_type=MESH,
         )
 
     wait_all(tot, 1)
-    lanes = pl.ds(pl.multiple_of((me // 2) * 128, 128), 128)
     everyone = in_three(tot[...].reshape(nctx, 128), iota((nctx, 128), 1) // 32)
-    fade[...] = jnp.exp(dot(everyone, oh[:, lanes])).reshape(nctx, 1, 128)
+    fade[...] = jnp.exp(dot(everyone, oh[:, my_lanes])).reshape(nctx, 1, 128)
 
     wait_all(slab_r, 3)
 
@@ -353,41 +353,44 @@
 
     for k in range(1, nctx):
         back_copy(lax.rem(me + k, nctx)).start()
-    inc[
-        pl.ds(pl.multiple_of(lax.rem(me, 2) * SLAB, SLAB), SLAB),
-        pl.ds(pl.multiple_of((me // 2) * 128, 128), 128),
-    ] = ret_s[me]
+    inc[my_rows, my_lanes] = ret_s[me]
 
     loads[6].wait()
 
     def gate_block(i, _):
         cols = columns(i // 4)
         at = pl.ds(pl.multiple_of(lax.rem(i, 4) * 128, 128), 128)
-        ab[at, cols] = dot(e3[at, :], oh[:, cols]) * silu(gateb[at, cols].astype(F32))
+        gate = dot(e3[at, :], oh[:, cols]) * silu(gateb[at, cols].astype(F32))
+        yb[at, cols] = yb[at, cols] * gate
+        ab[at, cols] = gate * rowsb[1:2, cols]
         return 0
 
     lax.fori_loop(0, ncb * 4, gate_block, 0)
     loads[7].wait()
     loads[8].wait()
 
-    wait_all(ret_s, 5)
+    def group_here(g):
+        for own_one in range(2):
+
+            @pl.when((group_me == g) if own_one else (group_me != g))
+            def _():
+                some = ret_s.at[pl.ds(0, nctx // GROUPS - own_one)]
+                pltpu.make_async_copy(some, some, csem.at[5 + g]).wait()
 
     group_n = iota((BLOCK, 128), 1) // 32
 
     def block_rows(b):
         return pl.ds(pl.multiple_of(b * BLOCK, BLOCK), BLOCK)
 
-    def norm_block(b):
-        at = block_rows(b)
+    def norm(at, blocks):
         mean = jnp.zeros((BLOCK, 128), F32)
-        for cb in range(ncb):
+        for cb in blocks:
             cols = slice(cb * COLS, (cb + 1) * COLS)
-            y = dot(qb[at, :], inc[:, cols]) * rowsb[1:2, cols] + yb[at, cols]
-            y = y * ab[at, cols]
+            y = dot(qb[at, :], inc[:, cols]) * ab[at, cols] + yb[at, cols]
             yb[at, cols] = y
             mean = mean + dot((y * y).astype(BF16), oht[cols, :])
         scale = in_three(lax.rsqrt(mean + 1e-05), group_n)
-        for cb in range(ncb):
+        for cb in blocks:
             cols = slice(cb * COLS, (cb + 1) * COLS)
             xb[at, cols] = (yb[at, cols] * dot(scale, oh[:, cols]) * gainb[:, cols]).astype(BF16)
 
@@ -409,8 +412,25 @@
             device_id_type=MESH,
         )
 
+    for g in range(2):
+        group_here(2 * g)
+        group_here(2 * g + 1)
+        norm(slice(0, BLOCK), range(g * ncb // 2, (g + 1) * ncb // 2))
+        feats_g = slice(g * feats // 2, (g + 1) * feats // 2)
+        for side in range(2):
+            at = lax.rem(z + 2, nhead) * outs + side * half_o
+            cols = pl.ds(pl.multiple_of(at, half_o), half_o)
+            part = dot(xb[0:BLOCK, feats_g], wb[feats_g, cols])
+            if g > 0:
+                part = part + own[side, 0]
+            if g < 1:
+                own[side, 0] = part
+            else:
+                rel_s[side, 0] = part.astype(BF16)
+                job_copy(rel_s, rel_r, side, 0, 0).start()
+
     def relay_block(b, _):
-        norm_block(b)
+        norm(block_rows(b), range(ncb))
 
         def one(side, _):
             rel_s[side, b] = project(b, lax.rem(z + 2, nhead), side).astype(BF16)
@@ -419,7 +439,7 @@
 
         return lax.fori_loop(0, 2, one, 0)
 
-    lax.fori_loop(0, nblk, relay_block, 0)
+    lax.fori_loop(1, nblk, relay_block, 0)
 
     def plain(i, _):
         b, side = i // 2, lax.rem(i, 2)
@@ -536,7 +556,7 @@
         vmem(job, F32),
         dma((9,)),
         dma((4,)),
-        dma((6,)),
+        dma((5 + GROUPS,)),
         dma((6 * (tokens // BLOCK),)),
         dma((6 * (tokens // BLOCK),)),
     ]

time: 67.7 us -> 67.4 us (level)
  Pallas kernels: 66.6 us -> 65.9 us
    pallas_call x1, Pallas kernels: 66.6 us -> 65.9 us  [per_device(): pl.pallas_call(functools.partial(layer, nctx, nhead), out_shape=jax.Shape...]
where the time goes in v2:
time: 67.4 us; the launch traced here: 66.9 us
  Pallas kernels  65.9 us (98%)
  local copies, waits for them, and re-layouts  0.97 us (1%)
    pallas_call x1, Pallas kernels, per_device(): pl.pallas_call(functools.partial(layer, nctx, nhead), out_shape=jax.Shape...  65.9 us

profile of v2, /device:TPU:1, one launch (start us, length us, event | category | flops | bytes accessed | tf_op | source)
XLA Modules:
  0.0 66.9 jit_solution(1004052231109385284)
XLA Ops:
  0.0 65.9 %ssd_layer.1 = bf16[512,1024]{1,0:T(8,128)(2,1)S(1)} custom-call(bf16[512,2048]{1,0:T(8,128)(2,1)} %feat_h.1, bf16[512,2048]{1,0:T(8,128)(2,1)} %gate_h.1, bf16[512,256]{1,0:T(8,128)(2,1)} %st_h.1, f32[32,512]{1,0:T(8,128)} %bitcast.3, f32[1,32]{1,0:T(1,128)} %bitcast.5, f32[4,2048]{1,0:T(4,128)} %taps_h.1, f32[4,256]{1,0:T(4,128)} %staps_h.1, ...), custom_call_target="tpu_custom_call" | custom-call | tf_op jit(solution)/shard_map/ssd_layer/pallas_call | solution.py:563
  65.9 1.0 %copy.11 = bf16[512,1024]{1,0:T(8,128)(2,1)} copy(bf16[512,1024]{1,0:T(8,128)(2,1)S(1)} %ssd_layer.1) | data formatting | bytes 2097152

commit v3 on v2

--- a/solution.py
+++ b/solution.py
@@ -14,7 +14,7 @@
 BF16 = jnp.bfloat16
 
 LEAD = 16
-ROWS = 64
+ROWS = 128
 BLOCK = 128
 COLS = 256
 SLAB = 64
@@ -349,7 +349,7 @@
             run = fade[i * 8 + e] * run + slab_r[i * 8 + e].astype(F32)
         return run
 
-    lax.fori_loop(0, nctx // 8, scan, jnp.zeros((SLAB, 128), F32))
+    lax.fori_loop(0, nctx // 8, scan, jnp.zeros((SLAB, 128), F32), unroll=True)
 
     for k in range(1, nctx):
         back_copy(lax.rem(me + k, nctx)).start()

time: 67.4 us -> 67.4 us (level)
  no operation moved by 1% of the time
where the time goes in v3:
time: 67.4 us; the launch traced here: 66.8 us
  Pallas kernels  65.9 us (98%)
  local copies, waits for them, and re-layouts  0.97 us (1%)
    pallas_call x1, Pallas kernels, per_device(): pl.pallas_call(functools.partial(layer, nctx, nhead), out_shape=jax.Shape...  65.9 us

profile of v3, /device:TPU:1, one launch (start us, length us, event | category | flops | bytes accessed | tf_op | source)
XLA Modules:
  0.0 66.8 jit_solution(13183684841809751313)
XLA Ops:
  0.0 65.9 %ssd_layer.1 = bf16[512,1024]{1,0:T(8,128)(2,1)S(1)} custom-call(bf16[512,2048]{1,0:T(8,128)(2,1)} %feat_h.1, bf16[512,2048]{1,0:T(8,128)(2,1)} %gate_h.1, bf16[512,256]{1,0:T(8,128)(2,1)} %st_h.1, f32[32,512]{1,0:T(8,128)} %bitcast.3, f32[1,32]{1,0:T(1,128)} %bitcast.5, f32[4,2048]{1,0:T(4,128)} %taps_h.1, f32[4,256]{1,0:T(4,128)} %staps_h.1, ...), custom_call_target="tpu_custom_call" | custom-call | tf_op jit(solution)/shard_map/ssd_layer/pallas_call | solution.py:563
  65.9 1.0 %copy.11 = bf16[512,1024]{1,0:T(8,128)(2,1)} copy(bf16[512,1024]{1,0:T(8,128)(2,1)S(1)} %ssd_layer.1) | data formatting | bytes 2097152
